TPU v7x, 128 devices: a whole 4x4x4 slice. The times are simulated.
128 devices in a mesh: dom: 32 (over z, x, core), blk: 4 (over y).
Axes of the slice: x: 4, y: 4, z: 4, core: 2. Of those that a mesh axis runs over, the one named last changes fastest.
Arguments:
- displacement: float32 [16384, 96], P(('dom', 'blk')), may hold values from -6 to 6
- damage: float32 [16384, 96], P(('dom', 'blk')), may hold values from 0 to 0.95
- applied_load: float32 [16384, 96], P(('dom', 'blk')), may hold values from -300 to 300
- tangent: bfloat16 [16384, 5, 96, 96], P(('dom', 'blk')), may hold values from -0.625 to 0.625
- laplacian: bfloat16 [16384, 5, 96, 96], P(('dom', 'blk')), may hold values from -0.25 to 0.25
- block_columns: int32 [16384, 5], P(('dom', 'blk')), may hold values from 0 to 1023, as said below
- send_lists: int32 [32, 2, 256], P('dom'), may hold values from -1 to 511, as said below
- hist_mech: float32 [16384, 27, 96], P(('dom', 'blk')), may hold values from 0 to 200
- mech_dest: int32 [16384], P(('dom', 'blk')), may hold values from 0 to 16383, as said below
- strain_matrix: float32 [27, 96, 96], replicated, may hold values from -0.625 to 0.625
- quad_weight: float32 [27], replicated, may hold values from 0.018518519 to 0.055555556
Outputs:
- mech_out: float32 [16384, 96], P(('dom', 'blk'))
- dmg_out: float32 [16384, 96], P(('dom', 'blk'))
- norms: float32 [2], replicated
Inputs may be any that keep to these rules, and one draw needn't show every extreme that they name: mech_dest is a permutation of the block rows. The 128 rows of one device go to at most 2 rows of any one device (itself included), and that many are reached in every draw. `send_lists`: -1 marks an unused slot; used slots come first and name distinct rows of the group, numbered within the group. Group 0 lists nothing for the group below and the last group nothing for the group above. Some list uses all 256 slots. `block_columns`: entries of the ghost parts of the extended numbering name only used slots of the neighbours' lists, never those of a missing neighbour, and every used slot is named by some block row of the receiving group.
All inputs are finite; a program needn't handle non-finite values.
Results may differ from a plain program's by a relative error of at most 0.00047.
Values may be sent and summed in bfloat16 or wider, within the bound.
A program may use at most 128 MiB of HBM per device.

v0:
```python
import jax
import jax.numpy as jnp
from jax import lax
from jax.sharding import PartitionSpec as P


def padded(x, sides, width):
    for axis, dim in sides:
        peers, length = (lax.axis_size(axis), x.shape[dim])
        up = [(i, (i + 1) % peers) for i in range(peers - 1)]
        down = [(j, i) for i, j in up]
        last = lax.slice_in_dim(x, length - width, length, axis=dim)
        leading = lax.slice_in_dim(x, 0, width, axis=dim)
        before = lax.ppermute(last, axis, up)
        after = lax.ppermute(leading, axis, down)
        x = jnp.concatenate([before, x, after], axis=dim)
    return x


def on_device(
    displacement,
    damage,
    applied_load,
    tangent,
    laplacian,
    block_columns,
    send_lists,
    hist_mech,
    mech_dest,
    strain_matrix,
    quad_weight,
):
    row_count = displacement.shape[0]
    width = displacement.shape[1]
    devices = lax.axis_size(("dom", "blk"))
    capacity = row_count // devices + 1
    root_deg = jnp.sqrt((1.0 - damage) ** 2 + 0.001)
    fields = jnp.stack(
        [(root_deg * displacement).astype(jnp.bfloat16), damage.astype(jnp.bfloat16)]
    )
    group_fields = lax.all_gather(fields, "blk", axis=1, tiled=True)
    own_lists = send_lists[0]
    safe_index = jnp.maximum(own_lists, 0)
    picked = group_fields[:, safe_index]
    picked = jnp.where((own_lists >= 0)[None, :, :, None], picked, jnp.zeros((), jnp.bfloat16))
    framed = padded(picked, (("dom", 1),), 1)
    lower_ghost = framed[:, 0]
    upper_ghost = framed[:, 3]
    extended = jnp.concatenate([group_fields, lower_ghost, upper_ghost], axis=1)
    near_rows = extended[:, block_columns]
    mech_sum = jnp.einsum("ikrc,ikc->ir", tangent, near_rows[0], preferred_element_type=jnp.float32)
    diffuse = jnp.einsum(
        "ikrc,ikc->ir", laplacian, near_rows[1], preferred_element_type=jnp.float32
    )
    mech_res = root_deg * mech_sum - applied_load
    dest_device = mech_dest // row_count
    dest_slot = mech_dest % row_count
    dest_marks = (dest_device[:, None] == jnp.arange(devices, dtype=jnp.int32)[None, :]).astype(
        jnp.int32
    )
    slot_rank = jnp.sum(jnp.cumsum(dest_marks, axis=0) * dest_marks, axis=1) - 1
    bucket = dest_device * capacity + slot_rank
    slot_table = (
        jnp.full((devices * capacity,), -1, jnp.int32)
        .at[bucket]
        .set(dest_slot)
        .reshape(devices, capacity)
    )
    parcel = (
        jnp.zeros((devices * capacity,) + hist_mech.shape[1:], jnp.float32)
        .at[bucket]
        .set(hist_mech)
    )
    parcel = parcel.reshape((devices, capacity) + hist_mech.shape[1:])
    got_slots, got_rows = (
        lax.all_to_all(slot_table, ("dom", "blk"), split_axis=0, concat_axis=0, tiled=True),
        lax.all_to_all(parcel, ("dom", "blk"), split_axis=0, concat_axis=0, tiled=True),
    )
    target = jnp.where(got_slots >= 0, got_slots, row_count).reshape(-1)
    history = (
        jnp.zeros_like(hist_mech)
        .at[target]
        .set(got_rows.reshape((-1,) + hist_mech.shape[1:]), mode="drop")
    )
    strain = jnp.einsum("qcr,ir->iqc", strain_matrix, displacement, precision=lax.Precision.HIGHEST)
    energy = 0.5 * strain * strain
    source = jnp.einsum(
        "q,iqc->ic", quad_weight, jnp.maximum(history, energy), precision=lax.Precision.HIGHEST
    )
    dmg_res = diffuse + (1.0 + 2.0 * source) * damage - 2.0 * source
    totals = lax.psum((jnp.sum(mech_res * mech_res), jnp.sum(dmg_res * dmg_res)), ("dom", "blk"))
    entries = row_count * width * devices
    mech_norm = jnp.sqrt(totals[0] / entries + 1e-06)
    dmg_norm = jnp.sqrt(totals[1] / entries + 1e-06)
    return (mech_res / mech_norm, dmg_res / dmg_norm, jnp.stack([mech_norm, dmg_norm]))


def solution(mesh):
    in_specs = (
        P(("dom", "blk"), None),
        P(("dom", "blk"), None),
        P(("dom", "blk"), None),
        P(("dom", "blk"), None, None, None),
        P(("dom", "blk"), None, None, None),
        P(("dom", "blk"), None),
        P("dom", None, None),
        P(("dom", "blk"), None, None),
        P(("dom", "blk")),
        P(),
        P(),
    )
    out_specs = (P(("dom", "blk"), None), P(("dom", "blk"), None), P())
    return jax.shard_map(
        on_device, mesh=mesh, in_specs=in_specs, out_specs=out_specs, check_vma=False
    )
```

profile of v0, /device:TPU:1, one launch (start us, length us, event | category | flops | bytes accessed | tf_op | source)
XLA Modules:
  0.0 223.9 jit_solution(6956331945346940331)
XLA Ops:
  0.6 0.0 copy-start
  0.6 0.0 copy-start.7
  0.7 0.0 copy-start.5
  0.7 0.8 maximum_bitcast_fusion
  1.5 0.7 compare_bitcast_fusion
  2.1 0.9 fusion.6
  3.1 11.1 %all_gather.3 = bf16[2,512,96]{1,2,0:T(8,128)(2,1)S(1)} all-gather(bf16[2,128,96]{1,2,0:T(8,128)(2,1)S(1)} %pad_maximum_fusion.1), channel_id=1, replica_groups=mesh['dom'=32,'blk'=4] {'blk'}, dimensions={1}, use_global_device_ids=true | all-gather | bytes 245760 | tf_op jit(solution)/shard_map/all_gather | solution.py:41
  14.1 0.2 copy.42
  14.3 0.0 copy-start.1
  14.3 2.1 gather_fusion
  16.4 1.1 fusion.3
  17.5 0.9 fusion.11
  18.5 4.2 %collective-permute-start.1 = (bf16[2,1,256,96]{3,0,2,1:T(2,128)(2,1)}, bf16[2,1,256,96]{3,0,2,1:T(2,128)(2,1)}, u32[]{:S(2)}, u32[]{:S(2)}) collective-permute-start(bf16[2,1,256,96]{3,0,2,1:T(2,128)(2,1)} %get-tuple-element.13), channel_id=1, source_target_pairs={{4,0},{8,4},{12,8},{16,12},{20,16},{24,20},{28,24},{32,28},{36,32}... | collective-permute-start | bytes 294920 | tf_op jit(solution)/shard_map/ppermute | solution.py:15
  22.7 3.0 %collective-permute-start = (bf16[2,1,256,96]{3,0,2,1:T(2,128)(2,1)}, bf16[2,1,256,96]{3,0,2,1:T(2,128)(2,1)}, u32[]{:S(2)}, u32[]{:S(2)}) collective-permute-start(bf16[2,1,256,96]{3,0,2,1:T(2,128)(2,1)} %get-tuple-element.12), channel_id=1, source_target_pairs={{0,4},{4,8},{8,12},{12,16},{16,20},{20,24},{24,28},{28,32},{32,36}... | collective-permute-start | bytes 294920 | tf_op jit(solution)/shard_map/ppermute | solution.py:14
  25.7 0.0 copy-done.7
  25.7 0.1 fusion.4
  25.8 0.2 reduce_window_sum.11
  26.0 0.2 select_reduce_fusion
  26.2 1.0 scatter_custom_fusion
  27.2 0.8 all_to_all.11
  27.9 9.0 %all-to-all-start = ((s32[128,1,2]{2,1,0:T(1,128)}), s32[128,1,2]{2,1,0:T(1,128)S(1)}, u32[]{:S(2)}, u32[]{:S(2)}) async-start(s32[128,1,2]{2,1,0:T(1,128)} %bitcast.20), calls=%async_computation | async-start | bytes 131072 | tf_op jit(solution)/shard_map/all_to_all | solution.py:76
  36.9 0.0 copy-done.5
  36.9 0.1 copy.43
  37.0 0.2 reshape.78
  37.2 0.0 copy-done.1
  37.2 2.3 %copy.47 = f32[128,27,96]{2,1,0:T(8,128)S(1)} copy(f32[128,27,96]{0,2,1:T(8,128)} %param.18) | data formatting | bytes 2654208 | tf_op args[7]
  39.5 2.5 %broadcast_in_dim.44 = f32[256,27,96]{2,1,0:T(8,128)} broadcast(f32[]{:T(128)} %constant.30.clone.1), dimensions={} | broadcast | bytes 2654212 | tf_op jit(solution)/shard_map/broadcast_in_dim | solution.py:70
  42.0 15.7 %scatter_fusion = f32[256,27,96]{2,1,0:T(8,128)} fusion(f32[256,27,96]{2,1,0:T(8,128)} %broadcast_in_dim.44, s32[128]{0:T(128)S(1)} %compare_select_fusion.3, f32[128,27,96]{2,1,0:T(8,128)S(1)} %copy.47), kind=kCustom, calls=%fused_computation.3 | custom fusion | bytes 3981824 | tf_op jit(solution)/shard_map/scatter | solution.py:72
  57.7 7.4 %copy.49 = f32[128,2,27,96]{3,1,2,0:T(2,128)} copy(f32[128,2,27,96]{3,2,1,0:T(8,128)} %bitcast.49) | data formatting | bytes 5308416 | tf_op jit(solution)/shard_map/reshape | solution.py:74
  65.1 0.0 copy-start.2
  65.1 0.0 all-to-all-done
  65.1 10.2 %all-to-all-start.1 = ((f32[128,2,27,96]{3,1,2,0:T(2,128)}), f32[128,2,27,96]{3,1,2,0:T(2,128)}, u32[]{:S(2)}, u32[]{:S(2)}) async-start(f32[128,2,27,96]{3,1,2,0:T(2,128)} %copy.49), calls=%async_computation.1 | async-start | bytes 7077888 | tf_op jit(solution)/shard_map/all_to_all | solution.py:77
  75.4 0.5 broadcast.139
  75.9 0.8 reduce.7
  76.7 0.1 all_to_all.13
  76.8 0.0 collective-permute-done.1
  76.8 0.0 collective-permute-done
  76.9 0.0 copy-done.2
  76.9 1.8 pad_maximum_fusion
  78.7 2.8 %gather_fusion.1 = bf16[640,2,96]{2,1,0:T(2,128)(2,1)S(1)} fusion(bf16[2,1024,96]{2,0,1:T(2,128)(2,1)S(1)} %pad_maximum_fusion, s32[1024]{0:T(1024)S(1)} %pad_clamp_fusion), kind=kCustom, calls=%fused_computation.1 | custom fusion | bytes 494080 | tf_op jit(solution)/shard_map/gather | solution.py:50
  81.5 0.5 fusion.10
  82.0 0.2 copy.77
  82.2 0.2 copy.76
  82.4 11.1 %multiply_reduce_fusion = (f32[128,96]{0,1:T(8,128)S(1)}, f32[128,96]{0,1:T(8,128)S(1)}) fusion(f32[128,96,5]{0,1,2:T(8,128)S(1)} %bitcast_convert_fusion, bf16[128,5,96,96]{0,3,2,1:T(8,128)(2,1)} %param.15, bf16[128,5,96,96]{0,3,2,1:T(8,128)(2,1)} %param.14, f32[128,96,5]{0,1,2:T(8,128)S(1)} %bitcast_convert_fusion.1), kind=kLoop, calls=%fused_computation.5 | loop fusion | flops 35364864 | bytes 24182784 | tf_op jit(solution)/shard_map/ikrc,ikc->ir/dot_general | solution.py:52
  93.5 27.7 %all-to-all-done.1 = f32[128,2,27,96]{3,1,2,0:T(2,128)} async-done(((f32[128,2,27,96]{3,1,2,0:T(2,128)}), f32[128,2,27,96]{3,1,2,0:T(2,128)}, u32[]{:S(2)}, u32[]{:S(2)}) %all-to-all-start.1) | async-done | bytes 2654240 | tf_op jit(solution)/shard_map/all_to_all | solution.py:77
  121.2 3.9 %copy.50 = f32[128,2,27,96]{3,1,0,2:T(2,128)S(1)} copy(f32[128,2,27,96]{3,1,2,0:T(2,128)} %all-to-all-done.1) | data formatting | bytes 5308416 | tf_op jit(solution)/shard_map/all_to_all | solution.py:77
  125.2 4.0 %copy.51 = f32[256,27,96]{2,1,0:T(8,128)} copy(f32[256,27,96]{2,0,1:T(8,128)S(1)} %bitcast.50) | data formatting | bytes 5308416 | tf_op jit(solution)/shard_map/reshape | solution.py:83
  129.2 0.2 broadcast_in_dim.40
  129.4 22.2 %scatter_fusion.1 = f32[128,27,96]{2,1,0:T(8,128)S(1)} fusion(f32[128,27,96]{2,1,0:T(8,128)S(1)} %broadcast_in_dim.40, s32[256]{0:T(256)S(1)} %bitcast.56, f32[256,27,96]{2,1,0:T(8,128)} %copy.51), kind=kCustom, calls=%fused_computation.4 | custom fusion | bytes 7963648 | tf_op jit(solution)/shard_map/scatter | solution.py:83
  151.7 1.8 copy.52
  153.5 0.0 copy-done
  153.5 0.0 copy-start.6
  153.5 0.0 copy-start.3
  153.5 0.0 copy-start.4
  153.5 2.6 %fusion.2 = f32[128,27,96]{0,2,1:T(8,128)S(1)} fusion(f32[128,27,96]{0,2,1:T(8,128)} %copy.52, f32[27,96,96]{2,1,0:T(8,128)S(1)} %copy-done, f32[128,96]{0,1:T(8,128)} %param.11), kind=kOutput, calls=%fused_computation.10 | convolution fusion | flops 383201280 | bytes 3698688 | tf_op jit(solution)/shard_map/qcr,ir->iqc/dot_general | solution.py:85
  156.1 0.0 copy-done.6
  156.1 1.8 fusion
  157.9 0.0 copy-done.3
  157.9 0.0 copy-done.4
  157.9 0.6 multiply_reduce_fusion.2
  158.6 62.7 %all-reduce = (f32[]{:T(128)}, f32[]{:T(128)}) all-reduce(f32[]{:T(128)} %get-tuple-element.7, f32[]{:T(128)} %get-tuple-element.6), channel_id=1, replica_groups=mesh['dom'=32,'blk'=4] {'dom','blk'}, use_global_device_ids=true, to_apply=%region_1.2 | all-reduce | flops 2 | bytes 16 | tf_op jit(solution)/shard_map/psum | solution.py:91
  222.7 0.7 broadcast_divide_fusion
  223.3 0.6 pad_maximum_fusion.2
  (10 shorter events, 0.1 us)
Async XLA Ops:
  0.6 152.8 %copy-start = (f32[27,96,96]{2,1,0:T(8,128)S(1)}, f32[27,96,96]{2,1,0:T(8,128)}, u32[]{:S(2)}) copy-start(f32[27,96,96]{2,1,0:T(8,128)} %param.20) | copy-start | bytes 2985988
  0.6 25.1 %copy-start.7 = (s32[128]{0:T(128)S(1)}, s32[128]{0:T(128)}, u32[]{:S(2)}) copy-start(s32[128]{0:T(128)} %param.19) | copy-start | bytes 1540
  0.7 36.2 %copy-start.5 = (s32[128,5]{0,1:T(8,128)S(1)}, s32[128,5]{0,1:T(8,128)}, u32[]{:S(2)}) copy-start(s32[128,5]{0,1:T(8,128)} %param.16) | copy-start | bytes 7684
  14.3 22.9 %copy-start.1 = (bf16[2,512,96]{2,0,1:T(2,128)(2,1)}, bf16[2,512,96]{2,0,1:T(2,128)(2,1)S(1)}, u32[]{:S(2)}) copy-start(bf16[2,512,96]{2,0,1:T(2,128)(2,1)S(1)} %copy.42) | copy-start | bytes 589828
  18.5 58.4 %collective-permute-start.1 = (bf16[2,1,256,96]{3,0,2,1:T(2,128)(2,1)}, bf16[2,1,256,96]{3,0,2,1:T(2,128)(2,1)}, u32[]{:S(2)}, u32[]{:S(2)}) collective-permute-start(bf16[2,1,256,96]{3,0,2,1:T(2,128)(2,1)} %get-tuple-element.13), channel_id=1, source_target_pairs={{4,0},{8,4},{12,8},{16,12},{20,16},{24,20},{28,24},{32,28},{36,32}... | collective-permute-start | bytes 294920 | tf_op jit(solution)/shard_map/ppermute | solution.py:15
  22.7 54.2 %collective-permute-start = (bf16[2,1,256,96]{3,0,2,1:T(2,128)(2,1)}, bf16[2,1,256,96]{3,0,2,1:T(2,128)(2,1)}, u32[]{:S(2)}, u32[]{:S(2)}) collective-permute-start(bf16[2,1,256,96]{3,0,2,1:T(2,128)(2,1)} %get-tuple-element.12), channel_id=1, source_target_pairs={{0,4},{4,8},{8,12},{12,16},{16,20},{20,24},{24,28},{28,32},{32,36}... | collective-permute-start | bytes 294920 | tf_op jit(solution)/shard_map/ppermute | solution.py:14
  27.9 37.2 %all-to-all-start = ((s32[128,1,2]{2,1,0:T(1,128)}), s32[128,1,2]{2,1,0:T(1,128)S(1)}, u32[]{:S(2)}, u32[]{:S(2)}) async-start(s32[128,1,2]{2,1,0:T(1,128)} %bitcast.20), calls=%async_computation | async-start | bytes 131072 | tf_op jit(solution)/shard_map/all_to_all | solution.py:76
  65.1 11.7 %copy-start.2 = (bf16[2,512,96]{2,0,1:T(2,128)(2,1)S(1)}, bf16[2,512,96]{2,0,1:T(2,128)(2,1)}, u32[]{:S(2)}) copy-start(bf16[2,512,96]{2,0,1:T(2,128)(2,1)} %copy-done.1) | copy-start | bytes 589828
  65.1 56.1 %all-to-all-start.1 = ((f32[128,2,27,96]{3,1,2,0:T(2,128)}), f32[128,2,27,96]{3,1,2,0:T(2,128)}, u32[]{:S(2)}, u32[]{:S(2)}) async-start(f32[128,2,27,96]{3,1,2,0:T(2,128)} %copy.49), calls=%async_computation.1 | async-start | bytes 7077888 | tf_op jit(solution)/shard_map/all_to_all | solution.py:77
  153.5 2.6 %copy-start.6 = (f32[27]{0:T(128)S(1)}, f32[27]{0:T(128)}, u32[]{:S(2)}) copy-start(f32[27]{0:T(128)} %param.21) | copy-start | bytes 328
  153.5 4.4 %copy-start.3 = (f32[128,96]{0,1:T(8,128)S(1)}, f32[128,96]{0,1:T(8,128)}, u32[]{:S(2)}) copy-start(f32[128,96]{0,1:T(8,128)} %param.12) | copy-start | bytes 147460
  153.5 4.4 %copy-start.4 = (f32[128,96]{0,1:T(8,128)S(1)}, f32[128,96]{0,1:T(8,128)}, u32[]{:S(2)}) copy-start(f32[128,96]{0,1:T(8,128)} %param.13) | copy-start | bytes 147460
where the time goes:
time: 226 us; the launch traced here: 224 us
  blocking collectives  73.8 us (33%)
  local copies, waits for them, and re-layouts  69.6 us (31%)
  waiting for transfers between devices  27.7 us (12%)
  starting transfers between devices  26.4 us (12%)
  other arithmetic  19.6 us (9%)
  matrix products  4.4 us (2%)
  between operations  2.38 us (1%)
    psum x1, blocking collectives, on_device(): lax.psum((jnp.sum(mech_res * mech_res), jnp.sum(dmg_res * dmg_res)), ('do...  62.7 us
    all_to_all x1, waiting for transfers between devices, on_device(): lax.all_to_all(parcel, ('dom', 'blk'), split_axis=0, concat_axis=0, tiled...  27.7 us
    scatter x2, local copies, waits for them, and re-layouts, on_device(): history = jnp.zeros_like(hist_mech).at[target].set(got_rows.reshape((-1,)...  24 us
    scatter x1, local copies, waits for them, and re-layouts, on_device(): parcel = jnp.zeros((devices * capacity,) + hist_mech.shape[1:], jnp.float...  15.7 us
    dot_general x1, other arithmetic, on_device(): jnp.einsum('ikrc,ikc->ir', laplacian, near_rows[1], preferred_element_typ...  11.1 us
    all_gather x1, blocking collectives, on_device(): group_fields = lax.all_gather(fields, 'blk', axis=1, tiled=True)  11.1 us
    all_to_all x1, starting transfers between devices, on_device(): lax.all_to_all(parcel, ('dom', 'blk'), split_axis=0, concat_axis=0, tiled...  10.2 us
    all_to_all x1, starting transfers between devices, on_device(): lax.all_to_all(slot_table, ('dom', 'blk'), split_axis=0, concat_axis=0, t...  8.96 us
  transfers between devices with their start and end apart: 4, of which 1 were waited for; matrix products, arithmetic and copies ran while one was open for 21% of the time, Pallas kernels for 0%

commit v1 on v0

--- a/solution.py
+++ b/solution.py
@@ -88,7 +88,9 @@
         "q,iqc->ic", quad_weight, jnp.maximum(history, energy), precision=lax.Precision.HIGHEST
     )
     dmg_res = diffuse + (1.0 + 2.0 * source) * damage - 2.0 * source
-    totals = lax.psum((jnp.sum(mech_res * mech_res), jnp.sum(dmg_res * dmg_res)), ("dom", "blk"))
+    totals = (jnp.sum(mech_res * mech_res), jnp.sum(dmg_res * dmg_res))
+    for q in ("dom", "blk"):
+        totals = jax.lax.psum(totals, axis_name=q)
     entries = row_count * width * devices
     mech_norm = jnp.sqrt(totals[0] / entries + 1e-06)
     dmg_norm = jnp.sqrt(totals[1] / entries + 1e-06)

time: 226 us -> 235 us (1.040)
  blocking collectives: 73.8 us -> 81.9 us
    psum x1 -> x2, blocking collectives: 62.7 us -> 70.9 us  [on_device(): totals = jax.lax.psum(totals, axis_name=q)]
  transfers between devices with their start and end apart: 4 -> 4, of which waited for: 1 -> 1; matrix products, arithmetic and copies ran while one was open for 21% -> 20% of each run, Pallas kernels for 0% -> 0%
where the time goes in v1:
time: 235 us; the launch traced here: 232 us
  blocking collectives  81.9 us (35%)
  local copies, waits for them, and re-layouts  69.6 us (30%)
  waiting for transfers between devices  27.7 us (12%)
  starting transfers between devices  26.4 us (11%)
  other arithmetic  19.6 us (8%)
  matrix products  4.4 us (2%)
  between operations  2.38 us (1%)
    psum x2, blocking collectives, on_device(): totals = jax.lax.psum(totals, axis_name=q)  70.9 us
    all_to_all x1, waiting for transfers between devices, on_device(): lax.all_to_all(parcel, ('dom', 'blk'), split_axis=0, concat_axis=0, tiled...  27.7 us
    scatter x2, local copies, waits for them, and re-layouts, on_device(): history = jnp.zeros_like(hist_mech).at[target].set(got_rows.reshape((-1,)...  24 us
    scatter x1, local copies, waits for them, and re-layouts, on_device(): parcel = jnp.zeros((devices * capacity,) + hist_mech.shape[1:], jnp.float...  15.7 us
    dot_general x1, other arithmetic, on_device(): jnp.einsum('ikrc,ikc->ir', laplacian, near_rows[1], preferred_element_typ...  11.1 us
    all_gather x1, blocking collectives, on_device(): group_fields = lax.all_gather(fields, 'blk', axis=1, tiled=True)  11.1 us
    all_to_all x1, starting transfers between devices, on_device(): lax.all_to_all(parcel, ('dom', 'blk'), split_axis=0, concat_axis=0, tiled...  10.2 us
    all_to_all x1, starting transfers between devices, on_device(): lax.all_to_all(slot_table, ('dom', 'blk'), split_axis=0, concat_axis=0, t...  8.96 us
  transfers between devices with their start and end apart: 4, of which 1 were waited for; matrix products, arithmetic and copies ran while one was open for 20% of the time, Pallas kernels for 0%

profile of v1, /device:TPU:1, one launch (start us, length us, event | category | flops | bytes accessed | tf_op | source)
XLA Modules:
  0.0 232.1 jit_solution(13431532739425287816)
XLA Ops:
  0.6 0.0 copy-start
  0.6 0.0 copy-start.7
  0.7 0.0 copy-start.5
  0.7 0.8 maximum_bitcast_fusion
  1.5 0.7 compare_bitcast_fusion
  2.1 0.9 fusion.6
  3.1 11.1 %all_gather.3 = bf16[2,512,96]{1,2,0:T(8,128)(2,1)S(1)} all-gather(bf16[2,128,96]{1,2,0:T(8,128)(2,1)S(1)} %pad_maximum_fusion.1), channel_id=1, replica_groups=mesh['dom'=32,'blk'=4] {'blk'}, dimensions={1}, use_global_device_ids=true | all-gather | bytes 245760 | tf_op jit(solution)/shard_map/all_gather | solution.py:41
  14.1 0.2 copy.42
  14.3 0.0 copy-start.1
  14.3 2.1 gather_fusion
  16.4 1.1 fusion.3
  17.5 0.9 fusion.11
  18.5 4.2 %collective-permute-start.1 = (bf16[2,1,256,96]{3,0,2,1:T(2,128)(2,1)}, bf16[2,1,256,96]{3,0,2,1:T(2,128)(2,1)}, u32[]{:S(2)}, u32[]{:S(2)}) collective-permute-start(bf16[2,1,256,96]{3,0,2,1:T(2,128)(2,1)} %get-tuple-element.15), channel_id=1, source_target_pairs={{4,0},{8,4},{12,8},{16,12},{20,16},{24,20},{28,24},{32,28},{36,32}... | collective-permute-start | bytes 294920 | tf_op jit(solution)/shard_map/ppermute | solution.py:15
  22.7 3.0 %collective-permute-start = (bf16[2,1,256,96]{3,0,2,1:T(2,128)(2,1)}, bf16[2,1,256,96]{3,0,2,1:T(2,128)(2,1)}, u32[]{:S(2)}, u32[]{:S(2)}) collective-permute-start(bf16[2,1,256,96]{3,0,2,1:T(2,128)(2,1)} %get-tuple-element.14), channel_id=1, source_target_pairs={{0,4},{4,8},{8,12},{12,16},{16,20},{20,24},{24,28},{28,32},{32,36}... | collective-permute-start | bytes 294920 | tf_op jit(solution)/shard_map/ppermute | solution.py:14
  25.7 0.0 copy-done.7
  25.7 0.1 fusion.4
  25.8 0.2 reduce_window_sum.11
  26.0 0.2 select_reduce_fusion
  26.2 1.0 scatter_custom_fusion
  27.2 0.8 all_to_all.11
  27.9 9.0 %all-to-all-start = ((s32[128,1,2]{2,1,0:T(1,128)}), s32[128,1,2]{2,1,0:T(1,128)S(1)}, u32[]{:S(2)}, u32[]{:S(2)}) async-start(s32[128,1,2]{2,1,0:T(1,128)} %bitcast.20), calls=%async_computation | async-start | bytes 131072 | tf_op jit(solution)/shard_map/all_to_all | solution.py:76
  36.9 0.0 copy-done.5
  36.9 0.1 copy.43
  37.0 0.2 reshape.78
  37.2 0.0 copy-done.1
  37.2 2.3 copy.47
  39.5 2.5 %broadcast_in_dim.44 = f32[256,27,96]{2,1,0:T(8,128)} broadcast(f32[]{:T(128)} %constant.30.clone.1), dimensions={} | broadcast | bytes 2654212 | tf_op jit(solution)/shard_map/broadcast_in_dim | solution.py:70
  42.0 15.7 %scatter_fusion = f32[256,27,96]{2,1,0:T(8,128)} fusion(f32[256,27,96]{2,1,0:T(8,128)} %broadcast_in_dim.44, s32[128]{0:T(128)S(1)} %compare_select_fusion.3, f32[128,27,96]{2,1,0:T(8,128)S(1)} %copy.47), kind=kCustom, calls=%fused_computation.3 | custom fusion | bytes 3981824 | tf_op jit(solution)/shard_map/scatter | solution.py:72
  57.7 7.4 %copy.49 = f32[128,2,27,96]{3,1,2,0:T(2,128)} copy(f32[128,2,27,96]{3,2,1,0:T(8,128)} %bitcast.49) | data formatting | bytes 5308416 | tf_op jit(solution)/shard_map/reshape | solution.py:74
  65.1 0.0 copy-start.2
  65.1 0.0 all-to-all-done
  65.1 10.2 %all-to-all-start.1 = ((f32[128,2,27,96]{3,1,2,0:T(2,128)}), f32[128,2,27,96]{3,1,2,0:T(2,128)}, u32[]{:S(2)}, u32[]{:S(2)}) async-start(f32[128,2,27,96]{3,1,2,0:T(2,128)} %copy.49), calls=%async_computation.1 | async-start | bytes 7077888 | tf_op jit(solution)/shard_map/all_to_all | solution.py:77
  75.4 0.5 broadcast.139
  75.9 0.8 reduce.7
  76.7 0.1 all_to_all.13
  76.8 0.0 collective-permute-done.1
  76.8 0.0 collective-permute-done
  76.9 0.0 copy-done.2
  76.9 1.8 pad_maximum_fusion
  78.7 2.8 %gather_fusion.1 = bf16[640,2,96]{2,1,0:T(2,128)(2,1)S(1)} fusion(bf16[2,1024,96]{2,0,1:T(2,128)(2,1)S(1)} %pad_maximum_fusion, s32[1024]{0:T(1024)S(1)} %pad_clamp_fusion), kind=kCustom, calls=%fused_computation.1 | custom fusion | bytes 494080 | tf_op jit(solution)/shard_map/gather | solution.py:50
  81.5 0.5 fusion.10
  82.0 0.2 copy.77
  82.2 0.2 copy.76
  82.4 11.1 %multiply_reduce_fusion = (f32[128,96]{0,1:T(8,128)S(1)}, f32[128,96]{0,1:T(8,128)S(1)}) fusion(f32[128,96,5]{0,1,2:T(8,128)S(1)} %bitcast_convert_fusion, bf16[128,5,96,96]{0,3,2,1:T(8,128)(2,1)} %param.15, bf16[128,5,96,96]{0,3,2,1:T(8,128)(2,1)} %param.14, f32[128,96,5]{0,1,2:T(8,128)S(1)} %bitcast_convert_fusion.1), kind=kLoop, calls=%fused_computation.5 | loop fusion | flops 35364864 | bytes 24182784 | tf_op jit(solution)/shard_map/ikrc,ikc->ir/dot_general | solution.py:52
  93.5 27.7 %all-to-all-done.1 = f32[128,2,27,96]{3,1,2,0:T(2,128)} async-done(((f32[128,2,27,96]{3,1,2,0:T(2,128)}), f32[128,2,27,96]{3,1,2,0:T(2,128)}, u32[]{:S(2)}, u32[]{:S(2)}) %all-to-all-start.1) | async-done | bytes 2654240 | tf_op jit(solution)/shard_map/all_to_all | solution.py:77
  121.2 3.9 %copy.50 = f32[128,2,27,96]{3,1,0,2:T(2,128)S(1)} copy(f32[128,2,27,96]{3,1,2,0:T(2,128)} %all-to-all-done.1) | data formatting | bytes 5308416 | tf_op jit(solution)/shard_map/all_to_all | solution.py:77
  125.2 4.0 %copy.51 = f32[256,27,96]{2,1,0:T(8,128)} copy(f32[256,27,96]{2,0,1:T(8,128)S(1)} %bitcast.50) | data formatting | bytes 5308416 | tf_op jit(solution)/shard_map/reshape | solution.py:83
  129.2 0.2 broadcast_in_dim.40
  129.4 22.2 %scatter_fusion.1 = f32[128,27,96]{2,1,0:T(8,128)S(1)} fusion(f32[128,27,96]{2,1,0:T(8,128)S(1)} %broadcast_in_dim.40, s32[256]{0:T(256)S(1)} %bitcast.56, f32[256,27,96]{2,1,0:T(8,128)} %copy.51), kind=kCustom, calls=%fused_computation.4 | custom fusion | bytes 7963648 | tf_op jit(solution)/shard_map/scatter | solution.py:83
  151.7 1.8 copy.52
  153.5 0.0 copy-done
  153.5 0.0 copy-start.6
  153.5 0.0 copy-start.3
  153.5 0.0 copy-start.4
  153.5 2.6 %fusion.2 = f32[128,27,96]{0,2,1:T(8,128)S(1)} fusion(f32[128,27,96]{0,2,1:T(8,128)} %copy.52, f32[27,96,96]{2,1,0:T(8,128)S(1)} %copy-done, f32[128,96]{0,1:T(8,128)} %param.11), kind=kOutput, calls=%fused_computation.10 | convolution fusion | flops 383201280 | bytes 3698688 | tf_op jit(solution)/shard_map/qcr,ir->iqc/dot_general | solution.py:85
  156.1 0.0 copy-done.6
  156.1 1.8 fusion
  157.9 0.0 copy-done.3
  157.9 0.0 copy-done.4
  157.9 0.6 multiply_reduce_fusion.2
  158.6 62.5 %all-reduce = (f32[]{:T(128)}, f32[]{:T(128)}) all-reduce(f32[]{:T(128)} %get-tuple-element.7, f32[]{:T(128)} %get-tuple-element.6), channel_id=1, replica_groups=mesh['dom'=32,'blk'=4] {'dom'}, use_global_device_ids=true, to_apply=%region_1.2 | all-reduce | flops 2 | bytes 16 | tf_op jit(solution)/shard_map/psum | solution.py:93
  221.1 8.3 %all-reduce.1 = (f32[]{:T(128)}, f32[]{:T(128)}) all-reduce(f32[]{:T(128)} %get-tuple-element.8, f32[]{:T(128)} %get-tuple-element.9), channel_id=1, replica_groups=mesh['dom'=32,'blk'=4] {'blk'}, use_global_device_ids=true, to_apply=%region_2.3 | all-reduce | flops 2 | bytes 16 | tf_op jit(solution)/shard_map/psum | solution.py:93
  230.8 0.7 broadcast_divide_fusion
  231.5 0.6 pad_maximum_fusion.2
  (10 shorter events, 0.1 us)
Async XLA Ops:
  0.6 152.8 %copy-start = (f32[27,96,96]{2,1,0:T(8,128)S(1)}, f32[27,96,96]{2,1,0:T(8,128)}, u32[]{:S(2)}) copy-start(f32[27,96,96]{2,1,0:T(8,128)} %param.20) | copy-start | bytes 2985988
  0.6 25.1 %copy-start.7 = (s32[128]{0:T(128)S(1)}, s32[128]{0:T(128)}, u32[]{:S(2)}) copy-start(s32[128]{0:T(128)} %param.19) | copy-start | bytes 1540
  0.7 36.2 %copy-start.5 = (s32[128,5]{0,1:T(8,128)S(1)}, s32[128,5]{0,1:T(8,128)}, u32[]{:S(2)}) copy-start(s32[128,5]{0,1:T(8,128)} %param.16) | copy-start | bytes 7684
  14.3 22.9 %copy-start.1 = (bf16[2,512,96]{2,0,1:T(2,128)(2,1)}, bf16[2,512,96]{2,0,1:T(2,128)(2,1)S(1)}, u32[]{:S(2)}) copy-start(bf16[2,512,96]{2,0,1:T(2,128)(2,1)S(1)} %copy.42) | copy-start | bytes 589828
  18.5 58.4 %collective-permute-start.1 = (bf16[2,1,256,96]{3,0,2,1:T(2,128)(2,1)}, bf16[2,1,256,96]{3,0,2,1:T(2,128)(2,1)}, u32[]{:S(2)}, u32[]{:S(2)}) collective-permute-start(bf16[2,1,256,96]{3,0,2,1:T(2,128)(2,1)} %get-tuple-element.15), channel_id=1, source_target_pairs={{4,0},{8,4},{12,8},{16,12},{20,16},{24,20},{28,24},{32,28},{36,32}... | collective-permute-start | bytes 294920 | tf_op jit(solution)/shard_map/ppermute | solution.py:15
  22.7 54.2 %collective-permute-start = (bf16[2,1,256,96]{3,0,2,1:T(2,128)(2,1)}, bf16[2,1,256,96]{3,0,2,1:T(2,128)(2,1)}, u32[]{:S(2)}, u32[]{:S(2)}) collective-permute-start(bf16[2,1,256,96]{3,0,2,1:T(2,128)(2,1)} %get-tuple-element.14), channel_id=1, source_target_pairs={{0,4},{4,8},{8,12},{12,16},{16,20},{20,24},{24,28},{28,32},{32,36}... | collective-permute-start | bytes 294920 | tf_op jit(solution)/shard_map/ppermute | solution.py:14
  27.9 37.2 %all-to-all-start = ((s32[128,1,2]{2,1,0:T(1,128)}), s32[128,1,2]{2,1,0:T(1,128)S(1)}, u32[]{:S(2)}, u32[]{:S(2)}) async-start(s32[128,1,2]{2,1,0:T(1,128)} %bitcast.20), calls=%async_computation | async-start | bytes 131072 | tf_op jit(solution)/shard_map/all_to_all | solution.py:76
  65.1 11.7 %copy-start.2 = (bf16[2,512,96]{2,0,1:T(2,128)(2,1)S(1)}, bf16[2,512,96]{2,0,1:T(2,128)(2,1)}, u32[]{:S(2)}) copy-start(bf16[2,512,96]{2,0,1:T(2,128)(2,1)} %copy-done.1) | copy-start | bytes 589828
  65.1 56.1 %all-to-all-start.1 = ((f32[128,2,27,96]{3,1,2,0:T(2,128)}), f32[128,2,27,96]{3,1,2,0:T(2,128)}, u32[]{:S(2)}, u32[]{:S(2)}) async-start(f32[128,2,27,96]{3,1,2,0:T(2,128)} %copy.49), calls=%async_computation.1 | async-start | bytes 7077888 | tf_op jit(solution)/shard_map/all_to_all | solution.py:77
  153.5 2.6 %copy-start.6 = (f32[27]{0:T(128)S(1)}, f32[27]{0:T(128)}, u32[]{:S(2)}) copy-start(f32[27]{0:T(128)} %param.21) | copy-start | bytes 328
  153.5 4.4 %copy-start.3 = (f32[128,96]{0,1:T(8,128)S(1)}, f32[128,96]{0,1:T(8,128)}, u32[]{:S(2)}) copy-start(f32[128,96]{0,1:T(8,128)} %param.12) | copy-start | bytes 147460
  153.5 4.4 %copy-start.4 = (f32[128,96]{0,1:T(8,128)S(1)}, f32[128,96]{0,1:T(8,128)}, u32[]{:S(2)}) copy-start(f32[128,96]{0,1:T(8,128)} %param.13) | copy-start | bytes 147460
